TPU v7x, 256 devices: a whole 4x4x8 slice. The times are simulated.
256 devices in a mesh: grp: 8 (over z_hi, y), row: 32 (over z_lo, x, core).
Axes of the slice: x: 4, y: 4, z: 8 (z_hi: 2, z_lo: 4; z = z_hi * 4 + z_lo), core: 2. Of those that a mesh axis runs over, the one named last changes fastest.
Arguments:
- points: bfloat16 [524288, 128], P(('grp', 'row')), as said below
- centers: bfloat16 [8192, 128], replicated, as said below
- inner_factor: bfloat16 [8192, 8192], P('row'), as said below
- outer_factor: bfloat16 [8192, 8192], P('row'), as said below
- iterate: float32 [64, 8192], P(None, 'row'), may hold values from -6 to 6
- residual: float32 [64, 8192], P(None, 'row'), as said below
- direction: float32 [64, 8192], P(None, 'row'), as said below
Outputs:
- next_iterate: float32 [64, 8192], P(None, 'row')
- next_residual: float32 [64, 8192], P(None, 'row')
- next_direction: float32 [64, 8192], P(None, 'row')
Inputs may be any that keep to these rules, and one draw needn't show every extreme that they name: `inner_factor`: upper triangular: zero below the diagonal, positive on it. `outer_factor`: upper triangular: zero below the diagonal, positive on it. `residual`: finite real values. `direction`: finite real values. `points`: finite real values. `centers`: finite real values.
All inputs are finite; a program needn't handle non-finite values.
Results may differ from a plain program's by a relative error of at most 0.0056.
Values may be sent and summed in bfloat16 or wider, within the bound.
No kernel may reach another device: no remote copies, remote signals or barrier semaphores. Data moves between devices by JAX's collectives and lax.ppermute only.
A program may use at most 64 MiB of HBM per device.

v0:
```python
import jax
import jax.numpy as jnp
from jax import lax
from jax.sharding import PartitionSpec as P

ridge_weight = 0.5


def kernel_rows(block_points, centers, center_norms):
    point_wide = block_points.astype(jnp.float32)
    point_norms = jnp.sum(point_wide * point_wide, axis=1)
    cross_term = lax.dot_general(
        block_points, centers, (((1,), (1,)), ((), ())), preferred_element_type=jnp.float32
    )
    distance = point_norms[:, None] + center_norms[None, :] - 2.0 * cross_term
    return jnp.exp(distance * (-4.0 / block_points.shape[1])).astype(jnp.bfloat16)


def local(points, centers, inner_factor, outer_factor, iterate, residual, direction):
    contract_last = (((1,), (1,)), ((), ()))
    own_rows = inner_factor.shape[0]
    targets = direction.shape[0]
    direction_half = direction.astype(jnp.bfloat16)
    columns = inner_factor
    inner_term = lax.dot_general(
        lax.all_gather(direction_half, "row", axis=1, tiled=True),
        columns,
        contract_last,
        preferred_element_type=jnp.float32,
    )
    inner_half = inner_term.astype(jnp.bfloat16)
    columns = outer_factor
    outer_rows = lax.dot_general(
        lax.all_gather(inner_half, "row", axis=1, tiled=True),
        columns,
        contract_last,
        preferred_element_type=jnp.float32,
    )
    outer_half = lax.all_gather(outer_rows.astype(jnp.bfloat16), "row", axis=1, tiled=True)
    center_wide = centers.astype(jnp.float32)
    center_norms = jnp.sum(center_wide * center_wide, axis=1)
    local_points = points.shape[0]
    block_rows = min(512, local_points)
    point_blocks = points.reshape(local_points // block_rows, block_rows, points.shape[1])

    def one_block(carried, block_points):
        kernel_block = kernel_rows(block_points, centers, center_norms)
        fitted = lax.dot_general(
            outer_half, kernel_block, contract_last, preferred_element_type=jnp.float32
        ).astype(jnp.bfloat16)
        return (carried + jnp.dot(fitted, kernel_block, preferred_element_type=jnp.float32), None)

    partial_sums, _ = lax.scan(
        one_block, jnp.zeros((targets, centers.shape[0]), jnp.float32), point_blocks
    )
    summed_all = lax.psum(partial_sums, ("grp", "row"))
    own_normal = lax.dynamic_slice_in_dim(summed_all, lax.axis_index("row") * own_rows, own_rows, 1)
    normal_half = own_normal.astype(jnp.bfloat16)
    point_count = local_points * lax.axis_size("grp") * lax.axis_size("row")
    outer_terms = jnp.dot(normal_half, outer_factor, preferred_element_type=jnp.float32)
    shaped = (
        lax.psum_scatter(outer_terms, "row", scatter_dimension=1, tiled=True) / point_count
        + ridge_weight * inner_term
    )
    shaped_half = shaped.astype(jnp.bfloat16)
    inner_terms = jnp.dot(shaped_half, inner_factor, preferred_element_type=jnp.float32)
    operator_image = lax.psum_scatter(inner_terms, "row", scatter_dimension=1, tiled=True)
    old_norm = lax.psum(jnp.sum(residual * residual, axis=1), "row")
    curvature = lax.psum(jnp.sum(direction * operator_image, axis=1), "row")
    step_size = old_norm / curvature
    next_residual = residual - step_size[:, None] * operator_image
    new_norm = lax.psum(jnp.sum(next_residual * next_residual, axis=1), "row")
    next_iterate = iterate + step_size[:, None] * direction
    next_direction = next_residual + (new_norm / old_norm)[:, None] * direction
    return (next_iterate, next_residual, next_direction)


def solution(mesh):
    placed = (
        P(("grp", "row"), None),
        P(),
        P("row", None),
        P("row", None),
        P(None, "row"),
        P(None, "row"),
        P(None, "row"),
    )
    return jax.shard_map(
        local,
        mesh=mesh,
        in_specs=placed,
        out_specs=(P(None, "row"), P(None, "row"), P(None, "row")),
        check_vma=False,
    )
```

profile of v0, /device:TPU:1, one launch (start us, length us, event | category | flops | bytes accessed | tf_op | source)
XLA Modules:
  0.0 819.4 jit_solution(775019206389307324)
XLA Ops:
  7.2 0.0 all-gather.4.cloned.1.call-start
  7.2 1.5 convert_element_type.29
  8.7 0.0 all-gather.4.cloned.1.call-update
  8.7 0.0 all-gather.6.cloned.1.call-start
  8.7 66.0 %all-gather.4.cloned.1.call-done = bf16[64,8192]{1,0:T(8,128)(2,1)} async-done(((bf16[64,256]{1,0:T(8,128)(2,1)}), bf16[64,8192]{1,0:T(8,128)(2,1)}) %all-gather.4.cloned.1.call-update) | async-done | bytes 1048592 | tf_op jit(solution)/shard_map/all_gather | solution.py:26
  74.8 4.5 fusion.10
  79.3 0.0 all-gather.6.cloned.1.call-update
  79.3 0.0 all-gather.8.cloned.1.call-start
  79.4 59.4 %all-gather.6.cloned.1.call-done = bf16[64,8192]{1,0:T(8,128)(2,1)} async-done(((bf16[64,256]{1,0:T(8,128)(2,1)}), bf16[64,8192]{1,0:T(8,128)(2,1)}) %all-gather.6.cloned.1.call-update) | async-done | bytes 1048592 | tf_op jit(solution)/shard_map/all_gather | solution.py:34
  138.7 4.5 convolution_convert_fusion.1
  143.2 0.0 all-gather.8.cloned.1.call-update
  143.3 0.2 reduce-scatter.3.cloned.1.call-start
  143.5 2.7 multiply_reduce_fusion.1
  146.3 56.4 %all-gather.8.cloned.1.call-done = bf16[64,8192]{1,0:T(8,128)(2,1)} async-done(((bf16[64,256]{1,0:T(8,128)(2,1)}), bf16[64,8192]{1,0:T(8,128)(2,1)}) %all-gather.8.cloned.1.call-update) | async-done | bytes 1048592 | tf_op jit(solution)/shard_map/all_gather | solution.py:39
  202.7 87.9 %while.11 = (s32[]{:T(128)}, f32[64,8192]{1,0:T(8,128)S(1)}, bf16[4,512,128]{2,1,0:T(8,128)(2,1)}, f32[8192]{0:T(1024)S(1)}, bf16[8192,128]{1,0:T(8,128)(2,1)}, ...) while((s32[]{:T(128)}, f32[64,8192]{1,0:T(8,128)S(1)}, bf16[4,512,128]{2,1,0:T(8,128)(2,1)}, ...), condition=%wide.region_5.6_spmd.clone, body=%wide.region_3.0_spmd.clone.sunk | while | flops 2169732608 | bytes 28610700 | solution.py:53
  202.7 1.0 multiply_reduce_fusion.6
  203.7 0.0 copy-start
  203.7 9.0 %exponential_convert_fusion.2 = bf16[512,8192]{1,0:T(8,128)(2,1)} fusion(bf16[8192,128]{1,0:T(8,128)(2,1)} %get-tuple-element.134, f32[8192]{0:T(1024)S(1)} %get-tuple-element.133, f32[512]{0:T(512)S(1)} %multiply_reduce_fusion.6, bf16[4,512,128]{2,1,0:T(8,128)(2,1)} %get-tuple-element.132, s32[]{:T(128)S(6)} %copy.12), kind=kOutput, calls=%fused_computation.clone.1 | convolution fusion | flops 1094713344 | bytes 10651652 | tf_op jit(solution)/shard_map/while/body/eval_jaxpr/dot_general | solution.py:12
  212.8 0.0 copy-done
  212.8 11.9 %convolution_add_fusion.2 = f32[64,8192]{1,0:T(8,128)S(1)} fusion(bf16[512,8192]{1,0:T(8,128)(2,1)} %exponential_convert_fusion.2, f32[64,8192]{1,0:T(8,128)S(1)} %get-tuple-element.123, pred[]{:T(512)S(6)} %compare.3, bf16[64,8192]{1,0:T(8,128)(2,1)S(1)} %copy-done), kind=kOutput, calls=%fused_computation.1.clone.1 | convolution fusion | flops 1074823168 | bytes 13631489 | tf_op jit(solution)/shard_map/while/body/eval_jaxpr/dot_general | solution.py:51
  224.7 1.1 multiply_reduce_fusion.6
  225.7 0.0 copy-start
  225.7 9.0 %exponential_convert_fusion.2 = bf16[512,8192]{1,0:T(8,128)(2,1)} fusion(bf16[8192,128]{1,0:T(8,128)(2,1)} %get-tuple-element.134, f32[8192]{0:T(1024)S(1)} %get-tuple-element.133, f32[512]{0:T(512)S(1)} %multiply_reduce_fusion.6, bf16[4,512,128]{2,1,0:T(8,128)(2,1)} %get-tuple-element.132, s32[]{:T(128)S(6)} %copy.12), kind=kOutput, calls=%fused_computation.clone.1 | convolution fusion | flops 1094713344 | bytes 10651652 | tf_op jit(solution)/shard_map/while/body/eval_jaxpr/dot_general | solution.py:12
  234.8 0.0 copy-done
  234.8 11.9 %convolution_add_fusion.2 = f32[64,8192]{1,0:T(8,128)S(1)} fusion(bf16[512,8192]{1,0:T(8,128)(2,1)} %exponential_convert_fusion.2, f32[64,8192]{1,0:T(8,128)S(1)} %get-tuple-element.123, pred[]{:T(512)S(6)} %compare.3, bf16[64,8192]{1,0:T(8,128)(2,1)S(1)} %copy-done), kind=kOutput, calls=%fused_computation.1.clone.1 | convolution fusion | flops 1074823168 | bytes 13631489 | tf_op jit(solution)/shard_map/while/body/eval_jaxpr/dot_general | solution.py:51
  246.6 1.1 multiply_reduce_fusion.6
  247.7 0.0 copy-start
  247.7 9.0 %exponential_convert_fusion.2 = bf16[512,8192]{1,0:T(8,128)(2,1)} fusion(bf16[8192,128]{1,0:T(8,128)(2,1)} %get-tuple-element.134, f32[8192]{0:T(1024)S(1)} %get-tuple-element.133, f32[512]{0:T(512)S(1)} %multiply_reduce_fusion.6, bf16[4,512,128]{2,1,0:T(8,128)(2,1)} %get-tuple-element.132, s32[]{:T(128)S(6)} %copy.12), kind=kOutput, calls=%fused_computation.clone.1 | convolution fusion | flops 1094713344 | bytes 10651652 | tf_op jit(solution)/shard_map/while/body/eval_jaxpr/dot_general | solution.py:12
  256.7 0.0 copy-done
  256.7 11.9 %convolution_add_fusion.2 = f32[64,8192]{1,0:T(8,128)S(1)} fusion(bf16[512,8192]{1,0:T(8,128)(2,1)} %exponential_convert_fusion.2, f32[64,8192]{1,0:T(8,128)S(1)} %get-tuple-element.123, pred[]{:T(512)S(6)} %compare.3, bf16[64,8192]{1,0:T(8,128)(2,1)S(1)} %copy-done), kind=kOutput, calls=%fused_computation.1.clone.1 | convolution fusion | flops 1074823168 | bytes 13631489 | tf_op jit(solution)/shard_map/while/body/eval_jaxpr/dot_general | solution.py:51
  268.6 1.1 multiply_reduce_fusion.6
  269.7 0.0 copy-start
  269.7 9.0 %exponential_convert_fusion.2 = bf16[512,8192]{1,0:T(8,128)(2,1)} fusion(bf16[8192,128]{1,0:T(8,128)(2,1)} %get-tuple-element.134, f32[8192]{0:T(1024)S(1)} %get-tuple-element.133, f32[512]{0:T(512)S(1)} %multiply_reduce_fusion.6, bf16[4,512,128]{2,1,0:T(8,128)(2,1)} %get-tuple-element.132, s32[]{:T(128)S(6)} %copy.12), kind=kOutput, calls=%fused_computation.clone.1 | convolution fusion | flops 1094713344 | bytes 10651652 | tf_op jit(solution)/shard_map/while/body/eval_jaxpr/dot_general | solution.py:12
  278.7 0.0 copy-done
  278.7 11.9 %convolution_add_fusion.2 = f32[64,8192]{1,0:T(8,128)S(1)} fusion(bf16[512,8192]{1,0:T(8,128)(2,1)} %exponential_convert_fusion.2, f32[64,8192]{1,0:T(8,128)S(1)} %get-tuple-element.123, pred[]{:T(512)S(6)} %compare.3, bf16[64,8192]{1,0:T(8,128)(2,1)S(1)} %copy-done), kind=kOutput, calls=%fused_computation.1.clone.1 | convolution fusion | flops 1074823168 | bytes 13631489 | tf_op jit(solution)/shard_map/while/body/eval_jaxpr/dot_general | solution.py:51
  290.6 85.9 %all-reduce.2 = bf16[64,8192]{1,0:T(8,128)(2,1)S(1)} all-reduce(f32[64,8192]{1,0:T(8,128)S(1)} %get-tuple-element.35), channel_id=1, replica_groups=mesh['grp'=8,'row'=32] {'grp','row'}, use_global_device_ids=true, to_apply=%region_6.7 | all-reduce | flops 524288 | bytes 3145728 | tf_op jit(solution)/shard_map/psum | solution.py:56
  376.5 4.4 fusion.3
  380.9 0.0 reduce-scatter.3.cloned.1.call-update
  380.9 0.0 reduce-scatter.5.cloned.1.call-start
  380.9 139.3 %reduce-scatter.3.cloned.1.call-done = f32[64,256]{1,0:T(8,128)} async-done(((f32[64,8192]{1,0:T(8,128)}), f32[64,256]{1,0:T(8,128)}) %reduce-scatter.3.cloned.1.call-update) | async-done | bytes 65552 | tf_op jit(solution)/shard_map/reduce_scatter | solution.py:62
  520.3 0.0 copy-start.3
  520.3 0.0 copy-start.1
  520.3 0.0 copy-start.4
  520.3 4.5 fusion.4
  524.8 0.0 reduce-scatter.5.cloned.1.call-update
  524.8 0.0 copy-done.3
  524.8 0.1 multiply_reduce_fusion.4
  524.9 144.8 %reduce-scatter.5.cloned.1.call-done = f32[64,256]{1,0:T(8,128)} async-done(((f32[64,8192]{1,0:T(8,128)}), f32[64,256]{1,0:T(8,128)}) %reduce-scatter.5.cloned.1.call-update) | async-done | bytes 65552 | tf_op jit(solution)/shard_map/reduce_scatter | solution.py:67
  669.7 0.0 copy-done.1
  669.7 0.9 multiply_reduce_fusion.3
  670.7 72.6 %all-reduce = (f32[64]{0:T(128)S(1)}, f32[64]{0:T(128)S(1)}) all-reduce(f32[64]{0:T(128)S(1)} %multiply_reduce_fusion.4, f32[64]{0:T(128)S(1)} %multiply_reduce_fusion.3), channel_id=1, replica_groups=mesh['grp'=8,'row'=32] {'row'}, use_global_device_ids=true, to_apply=%region_1.2 | all-reduce | flops 128 | bytes 1024 | tf_op jit(solution)/shard_map/psum | solution.py:68
  743.2 1.0 multiply_reduce_fusion.2
  744.3 0.0 copy-start.2
  744.3 67.9 %psum.31 = f32[64]{0:T(128)S(1)} all-reduce(f32[64]{0:T(128)S(1)} %get-tuple-element.71), channel_id=1, replica_groups=mesh['grp'=8,'row'=32] {'row'}, use_global_device_ids=true, to_apply=%region_12.13 | all-reduce | flops 64 | bytes 512 | tf_op jit(solution)/shard_map/psum | solution.py:72
  812.1 0.0 copy-done.4
  812.1 0.7 multiply_add_fusion
  812.9 0.0 copy-done.2
  (3 shorter events, 0.0 us)
Async XLA Ops:
  7.2 67.6 %all-gather.4.cloned.1.call-start = ((), (), s32[]{:S(2)}) async-start(), calls=%async_computation.2 | async-start | bytes 1081344 | tf_op jit(solution)/shard_map/all_gather | solution.py:26
  8.7 130.0 %all-gather.6.cloned.1.call-start = ((), (), s32[]{:S(2)}) async-start(), calls=%async_computation.3 | async-start | bytes 1081344 | tf_op jit(solution)/shard_map/all_gather | solution.py:34
  79.3 123.4 %all-gather.8.cloned.1.call-start = ((), (), s32[]{:S(2)}) async-start(), calls=%async_computation.4 | async-start | bytes 1081344 | tf_op jit(solution)/shard_map/all_gather | solution.py:39
  143.3 377.0 %reduce-scatter.3.cloned.1.call-start = ((), (), s32[]{:S(2)}) async-start(), calls=%async_computation.5 | async-start | bytes 2162688 | tf_op jit(solution)/shard_map/reduce_scatter | solution.py:62
  203.7 9.1 %copy-start = (bf16[64,8192]{1,0:T(8,128)(2,1)S(1)}, bf16[64,8192]{1,0:T(8,128)(2,1)}, u32[]{:S(2)}) copy-start(bf16[64,8192]{1,0:T(8,128)(2,1)} %get-tuple-element.135) | copy-start | bytes 3145732 | tf_op jit(solution)/shard_map/while
  225.7 9.1 %copy-start = (bf16[64,8192]{1,0:T(8,128)(2,1)S(1)}, bf16[64,8192]{1,0:T(8,128)(2,1)}, u32[]{:S(2)}) copy-start(bf16[64,8192]{1,0:T(8,128)(2,1)} %get-tuple-element.135) | copy-start | bytes 3145732 | tf_op jit(solution)/shard_map/while
  247.7 9.1 %copy-start = (bf16[64,8192]{1,0:T(8,128)(2,1)S(1)}, bf16[64,8192]{1,0:T(8,128)(2,1)}, u32[]{:S(2)}) copy-start(bf16[64,8192]{1,0:T(8,128)(2,1)} %get-tuple-element.135) | copy-start | bytes 3145732 | tf_op jit(solution)/shard_map/while
  269.7 9.1 %copy-start = (bf16[64,8192]{1,0:T(8,128)(2,1)S(1)}, bf16[64,8192]{1,0:T(8,128)(2,1)}, u32[]{:S(2)}) copy-start(bf16[64,8192]{1,0:T(8,128)(2,1)} %get-tuple-element.135) | copy-start | bytes 3145732 | tf_op jit(solution)/shard_map/while
  380.9 288.8 %reduce-scatter.5.cloned.1.call-start = ((), (), s32[]{:S(2)}) async-start(), calls=%async_computation.6 | async-start | bytes 2162688 | tf_op jit(solution)/shard_map/reduce_scatter | solution.py:67
  520.3 4.5 copy-start.3
  520.3 149.4 %copy-start.1 = (f32[64,256]{1,0:T(8,128)S(1)}, f32[64,256]{1,0:T(8,128)}, u32[]{:S(2)}) copy-start(f32[64,256]{1,0:T(8,128)} %param.15) | copy-start | bytes 196612
  520.3 291.8 %copy-start.4 = (f32[64,256]{1,0:T(8,128)S(1)}, f32[64,256]{1,0:T(8,128)}, u32[]{:S(2)}) copy-start(f32[64,256]{1,0:T(8,128)} %param.13) | copy-start | bytes 196612
  744.3 68.6 %copy-start.2 = (f32[64,256]{1,0:T(8,128)}, f32[64,256]{1,0:T(8,128)S(1)}, u32[]{:S(2)}) copy-start(f32[64,256]{1,0:T(8,128)S(1)} %get-tuple-element.72) | copy-start | bytes 196612
Sparse Core Ops, SparseCore 0:
  10.3 64.4 all-gather.3
  79.4 59.2 all-gather.5
  143.4 59.2 all-gather.7
  381.0 139.2 reduce-scatter.2
  524.9 144.7 reduce-scatter.4
where the time goes:
time: 820 us; the launch traced here: 819 us
  waiting for transfers between devices  466 us (57%)
  blocking collectives  226 us (28%)
  matrix products  101 us (12%)
  between operations  13.8 us (2%)
  other arithmetic  11.2 us (1%)
    reduce_scatter x1, waiting for transfers between devices, local(): lax.psum_scatter(inner_terms, 'row', scatter_dimension=1, tiled=True)  145 us
    reduce_scatter x1, waiting for transfers between devices, local(): lax.psum_scatter(outer_terms, 'row', scatter_dimension=1, tiled=True)  139 us
    psum x1, blocking collectives, local(): summed_all = lax.psum(partial_sums, ('grp', 'row'))  85.9 us
    psum x1, blocking collectives, local(): old_norm = lax.psum(jnp.sum(residual * residual, axis=1), 'row')  72.6 us
    psum x1, blocking collectives, local(): new_norm = lax.psum(jnp.sum(next_residual * next_residual, axis=1), 'row')  67.9 us
    all_gather x1, waiting for transfers between devices, local(): lax.all_gather(direction_half, 'row', axis=1, tiled=True)  66 us
    all_gather x1, waiting for transfers between devices, local(): lax.all_gather(inner_half, 'row', axis=1, tiled=True)  59.4 us
    all_gather x1, waiting for transfers between devices, local(): lax.all_gather(outer_rows.astype(jnp.bfloat16), 'row', axis=1, tiled=True)  56.4 us
  transfers between devices with their start and end apart: 5, of which 5 were waited for; matrix products, arithmetic and copies ran while one was open for 0% of the time, Pallas kernels for 0%

commit v1 on v0

--- a/solution.py
+++ b/solution.py
@@ -53,7 +53,7 @@
     partial_sums, _ = lax.scan(
         one_block, jnp.zeros((targets, centers.shape[0]), jnp.float32), point_blocks
     )
-    summed_all = lax.psum(partial_sums, ("grp", "row"))
+    summed_all = lax.psum(lax.psum(partial_sums, "grp"), "row")
     own_normal = lax.dynamic_slice_in_dim(summed_all, lax.axis_index("row") * own_rows, own_rows, 1)
     normal_half = own_normal.astype(jnp.bfloat16)
     point_count = local_points * lax.axis_size("grp") * lax.axis_size("row")

time: 820 us -> 1020 us (1.24)
  waiting for transfers between devices: 466 us -> 604 us
  blocking collectives: 226 us -> 291 us
    psum x0 -> x1, waiting for transfers between devices: none -> 129 us  [local(): summed_all = lax.psum(lax.psum(partial_sums, 'grp'), 'row')]
    psum x1, blocking collectives: 85.9 us -> 150 us  [local(): summed_all = lax.psum(lax.psum(partial_sums, 'grp'), 'row')]
  transfers between devices with their start and end apart: 5 -> 6, of which waited for: 5 -> 6; matrix products, arithmetic and copies ran while one was open for 0% -> 0% of each run, Pallas kernels for 0% -> 0%
where the time goes in v1:
time: 1020 us
  waiting for transfers between devices  604 us (59%)
  blocking collectives  291 us (29%)
  matrix products  101 us (10%)
  between operations  14.2 us (1%)
  other arithmetic  11.2 us (1%)
    psum x1, blocking collectives, local(): summed_all = lax.psum(lax.psum(partial_sums, 'grp'), 'row')  150 us
    reduce_scatter x1, waiting for transfers between devices, local(): lax.psum_scatter(outer_terms, 'row', scatter_dimension=1, tiled=True)  148 us
    reduce_scatter x1, waiting for transfers between devices, local(): lax.psum_scatter(inner_terms, 'row', scatter_dimension=1, tiled=True)  145 us
    psum x1, waiting for transfers between devices, local(): summed_all = lax.psum(lax.psum(partial_sums, 'grp'), 'row')  129 us
    psum x1, blocking collectives, local(): old_norm = lax.psum(jnp.sum(residual * residual, axis=1), 'row')  72.6 us
    psum x1, blocking collectives, local(): new_norm = lax.psum(jnp.sum(next_residual * next_residual, axis=1), 'row')  67.9 us
    all_gather x1, waiting for transfers between devices, local(): lax.all_gather(direction_half, 'row', axis=1, tiled=True)  66 us
    all_gather x1, waiting for transfers between devices, local(): lax.all_gather(inner_half, 'row', axis=1, tiled=True)  59.4 us
  transfers between devices with their start and end apart: 6, of which 6 were waited for; matrix products, arithmetic and copies ran while one was open for 0% of the time, Pallas kernels for 0%

profile of v1, /device:TPU:1, one launch (start us, length us, event | category | flops | bytes accessed | tf_op | source)
XLA Modules:
  0.0 1023.1 jit_solution(1360982733832563381)
XLA Ops:
  7.2 0.0 all-gather.4.cloned.1.call-start
  7.2 1.5 convert_element_type.29
  8.7 0.0 all-gather.4.cloned.1.call-update
  8.7 0.0 all-gather.6.cloned.1.call-start
  8.7 66.0 %all-gather.4.cloned.1.call-done = bf16[64,8192]{1,0:T(8,128)(2,1)} async-done(((bf16[64,256]{1,0:T(8,128)(2,1)}), bf16[64,8192]{1,0:T(8,128)(2,1)}) %all-gather.4.cloned.1.call-update) | async-done | bytes 1048592 | tf_op jit(solution)/shard_map/all_gather | solution.py:26
  74.8 4.5 fusion.10
  79.3 0.0 all-gather.6.cloned.1.call-update
  79.3 0.0 all-gather.8.cloned.1.call-start
  79.4 59.4 %all-gather.6.cloned.1.call-done = bf16[64,8192]{1,0:T(8,128)(2,1)} async-done(((bf16[64,256]{1,0:T(8,128)(2,1)}), bf16[64,8192]{1,0:T(8,128)(2,1)}) %all-gather.6.cloned.1.call-update) | async-done | bytes 1048592 | tf_op jit(solution)/shard_map/all_gather | solution.py:34
  138.7 4.5 convolution_convert_fusion.1
  143.2 0.0 all-gather.8.cloned.1.call-update
  143.3 0.0 all-reduce.4.cloned.1.call-start
  143.3 2.7 multiply_reduce_fusion.1
  146.1 56.6 %all-gather.8.cloned.1.call-done = bf16[64,8192]{1,0:T(8,128)(2,1)} async-done(((bf16[64,256]{1,0:T(8,128)(2,1)}), bf16[64,8192]{1,0:T(8,128)(2,1)}) %all-gather.8.cloned.1.call-update) | async-done | bytes 1048592 | tf_op jit(solution)/shard_map/all_gather | solution.py:39
  202.7 87.9 %while.11 = (s32[]{:T(128)}, f32[64,8192]{1,0:T(8,128)S(1)}, bf16[4,512,128]{2,1,0:T(8,128)(2,1)}, f32[8192]{0:T(1024)S(1)}, bf16[8192,128]{1,0:T(8,128)(2,1)}, ...) while((s32[]{:T(128)}, f32[64,8192]{1,0:T(8,128)S(1)}, bf16[4,512,128]{2,1,0:T(8,128)(2,1)}, ...), condition=%wide.region_5.6_spmd.clone, body=%wide.region_3.0_spmd.clone.sunk | while | flops 2169732608 | bytes 28610700 | solution.py:53
  202.7 1.0 multiply_reduce_fusion.6
  203.7 0.0 copy-start.1
  203.7 9.1 exponential_convert_fusion.2
  212.8 0.0 copy-done.1
  212.8 11.9 %convolution_add_fusion.2 = f32[64,8192]{1,0:T(8,128)S(1)} fusion(bf16[512,8192]{1,0:T(8,128)(2,1)} %exponential_convert_fusion.2, f32[64,8192]{1,0:T(8,128)S(1)} %get-tuple-element.123, pred[]{:T(512)S(6)} %compare.3, bf16[64,8192]{1,0:T(8,128)(2,1)S(1)} %copy-done.1), kind=kOutput, calls=%fused_computation.1.clone.1 | convolution fusion | flops 1074823168 | bytes 13631489 | tf_op jit(solution)/shard_map/while/body/eval_jaxpr/dot_general | solution.py:51
  224.7 1.1 multiply_reduce_fusion.6
  225.7 0.0 copy-start.1
  225.7 9.0 exponential_convert_fusion.2
  234.8 0.0 copy-done.1
  234.8 11.9 %convolution_add_fusion.2 = f32[64,8192]{1,0:T(8,128)S(1)} fusion(bf16[512,8192]{1,0:T(8,128)(2,1)} %exponential_convert_fusion.2, f32[64,8192]{1,0:T(8,128)S(1)} %get-tuple-element.123, pred[]{:T(512)S(6)} %compare.3, bf16[64,8192]{1,0:T(8,128)(2,1)S(1)} %copy-done.1), kind=kOutput, calls=%fused_computation.1.clone.1 | convolution fusion | flops 1074823168 | bytes 13631489 | tf_op jit(solution)/shard_map/while/body/eval_jaxpr/dot_general | solution.py:51
  246.6 1.1 multiply_reduce_fusion.6
  247.7 0.0 copy-start.1
  247.7 9.0 exponential_convert_fusion.2
  256.8 0.0 copy-done.1
  256.8 11.9 %convolution_add_fusion.2 = f32[64,8192]{1,0:T(8,128)S(1)} fusion(bf16[512,8192]{1,0:T(8,128)(2,1)} %exponential_convert_fusion.2, f32[64,8192]{1,0:T(8,128)S(1)} %get-tuple-element.123, pred[]{:T(512)S(6)} %compare.3, bf16[64,8192]{1,0:T(8,128)(2,1)S(1)} %copy-done.1), kind=kOutput, calls=%fused_computation.1.clone.1 | convolution fusion | flops 1074823168 | bytes 13631489 | tf_op jit(solution)/shard_map/while/body/eval_jaxpr/dot_general | solution.py:51
  268.6 1.1 multiply_reduce_fusion.6
  269.7 0.0 copy-start.1
  269.7 9.0 exponential_convert_fusion.2
  278.7 0.0 copy-done.1
  278.7 11.9 %convolution_add_fusion.2 = f32[64,8192]{1,0:T(8,128)S(1)} fusion(bf16[512,8192]{1,0:T(8,128)(2,1)} %exponential_convert_fusion.2, f32[64,8192]{1,0:T(8,128)S(1)} %get-tuple-element.123, pred[]{:T(512)S(6)} %compare.3, bf16[64,8192]{1,0:T(8,128)(2,1)S(1)} %copy-done.1), kind=kOutput, calls=%fused_computation.1.clone.1 | convolution fusion | flops 1074823168 | bytes 13631489 | tf_op jit(solution)/shard_map/while/body/eval_jaxpr/dot_general | solution.py:51
  290.6 0.0 copy-start
  290.6 1.3 copy-done
  291.9 0.0 all-reduce.4.cloned.1.call-update
  291.9 0.0 reduce-scatter.3.cloned.1.call-start
  292.0 129.0 %all-reduce.4.cloned.1.call-done = f32[64,8192]{1,0:T(8,128)} async-done(((f32[64,8192]{1,0:T(8,128)}), f32[64,8192]{1,0:T(8,128)}) %all-reduce.4.cloned.1.call-update) | async-done | bytes 2097168 | tf_op jit(solution)/shard_map/psum | solution.py:56
  421.0 150.3 %all-reduce.5 = bf16[64,8192]{1,0:T(8,128)(2,1)S(1)} all-reduce(f32[64,8192]{1,0:T(8,128)} %all-reduce.4.cloned.1.call-done), channel_id=1, replica_groups=mesh['grp'=8,'row'=32] {'row'}, use_global_device_ids=true, to_apply=%region_7.8 | all-reduce | flops 524288 | bytes 3145728 | tf_op jit(solution)/shard_map/psum | solution.py:56
  571.3 4.4 fusion.3
  575.7 0.0 reduce-scatter.3.cloned.1.call-update
  575.8 0.0 reduce-scatter.5.cloned.1.call-start
  575.8 147.9 %reduce-scatter.3.cloned.1.call-done = f32[64,256]{1,0:T(8,128)} async-done(((f32[64,8192]{1,0:T(8,128)}), f32[64,256]{1,0:T(8,128)}) %reduce-scatter.3.cloned.1.call-update) | async-done | bytes 65552 | tf_op jit(solution)/shard_map/reduce_scatter | solution.py:62
  723.7 0.0 copy-start.4
  723.7 0.0 copy-start.2
  723.7 0.0 copy-start.5
  723.7 4.5 fusion.4
  728.1 0.0 reduce-scatter.5.cloned.1.call-update
  728.1 0.0 copy-done.4
  728.2 0.1 multiply_reduce_fusion.4
  728.3 144.8 %reduce-scatter.5.cloned.1.call-done = f32[64,256]{1,0:T(8,128)} async-done(((f32[64,8192]{1,0:T(8,128)}), f32[64,256]{1,0:T(8,128)}) %reduce-scatter.5.cloned.1.call-update) | async-done | bytes 65552 | tf_op jit(solution)/shard_map/reduce_scatter | solution.py:67
  873.1 0.0 copy-done.2
  873.1 0.9 multiply_reduce_fusion.3
  874.0 72.6 %all-reduce = (f32[64]{0:T(128)S(1)}, f32[64]{0:T(128)S(1)}) all-reduce(f32[64]{0:T(128)S(1)} %multiply_reduce_fusion.4, f32[64]{0:T(128)S(1)} %multiply_reduce_fusion.3), channel_id=1, replica_groups=mesh['grp'=8,'row'=32] {'row'}, use_global_device_ids=true, to_apply=%region_1.2 | all-reduce | flops 128 | bytes 1024 | tf_op jit(solution)/shard_map/psum | solution.py:68
  946.6 1.0 multiply_reduce_fusion.2
  947.6 0.0 copy-start.3
  947.6 67.9 %psum.39 = f32[64]{0:T(128)S(1)} all-reduce(f32[64]{0:T(128)S(1)} %get-tuple-element.71), channel_id=1, replica_groups=mesh['grp'=8,'row'=32] {'row'}, use_global_device_ids=true, to_apply=%region_13.14 | all-reduce | flops 64 | bytes 512 | tf_op jit(solution)/shard_map/psum | solution.py:72
  1015.5 0.0 copy-done.5
  1015.5 0.7 multiply_add_fusion
  1016.2 0.0 copy-done.3
  (3 shorter events, 0.0 us)
Async XLA Ops:
  7.2 67.6 %all-gather.4.cloned.1.call-start = ((), (), s32[]{:S(2)}) async-start(), calls=%async_computation.2 | async-start | bytes 1081344 | tf_op jit(solution)/shard_map/all_gather | solution.py:26
  8.7 130.0 %all-gather.6.cloned.1.call-start = ((), (), s32[]{:S(2)}) async-start(), calls=%async_computation.3 | async-start | bytes 1081344 | tf_op jit(solution)/shard_map/all_gather | solution.py:34
  79.3 123.4 %all-gather.8.cloned.1.call-start = ((), (), s32[]{:S(2)}) async-start(), calls=%async_computation.4 | async-start | bytes 1081344 | tf_op jit(solution)/shard_map/all_gather | solution.py:39
  143.3 277.8 %all-reduce.4.cloned.1.call-start = ((), (), s32[]{:S(2)}) async-start(), calls=%async_computation.5 | async-start | bytes 4194304 | tf_op jit(solution)/shard_map/psum | solution.py:56
  203.7 9.1 copy-start.1
  225.7 9.1 copy-start.1
  247.7 9.1 copy-start.1
  269.7 9.1 copy-start.1
  290.6 1.3 copy-start
  291.9 431.7 %reduce-scatter.3.cloned.1.call-start = ((), (), s32[]{:S(2)}) async-start(), calls=%async_computation.6 | async-start | bytes 2162688 | tf_op jit(solution)/shard_map/reduce_scatter | solution.py:62
  575.8 297.3 %reduce-scatter.5.cloned.1.call-start = ((), (), s32[]{:S(2)}) async-start(), calls=%async_computation.7 | async-start | bytes 2162688 | tf_op jit(solution)/shard_map/reduce_scatter | solution.py:67
  723.7 4.5 copy-start.4
  723.7 149.4 %copy-start.2 = (f32[64,256]{1,0:T(8,128)S(1)}, f32[64,256]{1,0:T(8,128)}, u32[]{:S(2)}) copy-start(f32[64,256]{1,0:T(8,128)} %param.15) | copy-start | bytes 196612
  723.7 291.8 %copy-start.5 = (f32[64,256]{1,0:T(8,128)S(1)}, f32[64,256]{1,0:T(8,128)}, u32[]{:S(2)}) copy-start(f32[64,256]{1,0:T(8,128)} %param.13) | copy-start | bytes 196612
  947.6 68.6 %copy-start.3 = (f32[64,256]{1,0:T(8,128)}, f32[64,256]{1,0:T(8,128)S(1)}, u32[]{:S(2)}) copy-start(f32[64,256]{1,0:T(8,128)S(1)} %get-tuple-element.72) | copy-start | bytes 196612
Sparse Core Ops, SparseCore 0:
  10.3 64.4 all-gather.3
  79.4 59.2 all-gather.5
  143.4 59.2 all-gather.7
  292.1 128.9 all-reduce.3
  575.9 147.7 reduce-scatter.2
  728.3 144.7 reduce-scatter.4
